TPU v7x, 32 devices: a whole 2x2x4 slice. The times are simulated.
32 devices in a mesh: dp: 8 (over z, y), tensor: 4 (over x, core).
Axes of the slice: x: 2, y: 2, z: 4, core: 2. Of those that a mesh axis runs over, the one named last changes fastest.
Arguments:
- layer_input_rows: bfloat16 [32768, 768], P(('dp', 'tensor')), may hold values from -6 to 6
- output_gradient: bfloat16 [32768, 768], P(('dp', 'tensor')), may hold values from -6 to 6
- query_weight: bfloat16 [768, 768], P('dp', 'tensor'), may hold values from -0.21875 to 0.21875
- key_weight: bfloat16 [768, 768], P('dp', 'tensor'), may hold values from -0.21875 to 0.21875
- value_weight: bfloat16 [768, 768], P('dp', 'tensor'), may hold values from -0.21875 to 0.21875
- output_weight: bfloat16 [768, 768], P('tensor', 'dp'), may hold values from -1.75 to 1.75
- up_weight: bfloat16 [768, 3072], P('dp', 'tensor'), may hold values from -0.21875 to 0.21875
- down_weight: bfloat16 [3072, 768], P('tensor', 'dp'), may hold values from -0.109375 to 0.109375
- query_bias_vector: float32 [768], P('tensor'), may hold values from -3 to 3
- value_bias_vector: float32 [768], P('tensor'), may hold values from -3 to 3
- output_bias_vector: float32 [768], replicated, may hold values from -5 to 5
- up_bias_vector: float32 [3072], P('tensor'), may hold values from -3 to 3
- down_bias_vector: float32 [768], replicated, may hold values from -2 to 2
- query_down_frozen: bfloat16 [768, 8], replicated, may hold values from -0.21875 to 0.21875
- value_down_frozen: bfloat16 [768, 8], replicated, may hold values from -0.21875 to 0.21875
- query_up_trained: bfloat16 [8, 768], P(None, 'tensor'), may hold values from -0.59765625 to 0.59765625
- value_up_trained: bfloat16 [8, 768], P(None, 'tensor'), may hold values from -0.59765625 to 0.59765625
- first_norm_gain: float32 [768], replicated, may hold values from 0.5 to 1.5
- first_norm_bias: float32 [768], replicated, may hold values from -2 to 2
- second_norm_gain: float32 [768], replicated, may hold values from 0.5 to 1.5
- second_norm_bias: float32 [768], replicated, may hold values from -2 to 2
- segments: int32 [32768], P('dp'), may hold values from 0 to 48, as said below
- sentence_row_mask: int32 [32768], P('dp'), may hold values from 0 to 1, as said below
Outputs:
- output: bfloat16 [32768, 768], P(('dp', 'tensor'))
- grad_input: bfloat16 [32768, 768], P(('dp', 'tensor'))
- grad_lora_query: float32 [8, 768], P(None, 'tensor')
- grad_lora_value: float32 [8, 768], P(None, 'tensor')
Inputs may be any that keep to these rules, and one draw needn't show every extreme that they name: `segments`: ids restart at 0 in every sequence of 512 rows and rise by one at each sentence boundary; sentences hold 8 to 128 rows, and the first sentence of every sequence holds exactly 128 rows; in the first sequence of all rows every later sentence holds exactly 8 rows; the padding rows at a sequence's end share one more id. `sentence_row_mask`: in each sequence of 512 rows the rows after the last sentence that ends before row 512 are 0, from 1 to 128 of them; all others are 1.
All inputs are finite; a program needn't handle non-finite values.
Results may differ from a plain program's by a relative error of at most 0.02.
Values may be sent and summed in bfloat16 or wider, within the bound.
A program may use at most 128 MiB of HBM per device.

v0:
```python
import jax
import jax.numpy as jnp
from jax import lax
from jax.sharding import PartitionSpec as P

HEAD_DIM = 64
ADAPTER_RANK = 8
ADAPTER_NUMER = 16
SEQ = 512
EPSILON = 1e-05
NEG_FILL = -1e30
WIDE = jnp.float32
NARROW = jnp.bfloat16


def layer_norm(rows, gain, shift):
    mean = jnp.mean(rows, axis=-1, keepdims=True)
    centered = rows - mean
    variance = jnp.mean(centered * centered, axis=-1, keepdims=True)
    inverse = lax.rsqrt(variance + EPSILON)
    normed = centered * inverse
    return (normed * gain + shift, normed, inverse)


def norm_back(grad, normed, inverse, gain):
    scaled = grad * gain
    centered = scaled - jnp.mean(scaled, axis=-1, keepdims=True)
    return inverse * (centered - normed * jnp.mean(scaled * normed, axis=-1, keepdims=True))


def mm(left, right):
    return jnp.dot(left, right, preferred_element_type=WIDE)


def mm_nt(left, right):
    return lax.dot_general(left, right, (((1,), (1,)), ((), ())), preferred_element_type=WIDE)


def mm_tn(left, right):
    return lax.dot_general(left, right, (((0,), (0,)), ((), ())), preferred_element_type=WIDE)


def body(
    layer_input_rows,
    output_gradient,
    query_weight,
    key_weight,
    value_weight,
    output_weight,
    up_weight,
    down_weight,
    query_bias_vector,
    value_bias_vector,
    output_bias_vector,
    up_bias_vector,
    down_bias_vector,
    query_down_frozen,
    value_down_frozen,
    query_up_trained,
    value_up_trained,
    first_norm_gain,
    first_norm_bias,
    second_norm_gain,
    second_norm_bias,
    segments,
    sentence_row_mask,
):
    adapter_scale = ADAPTER_NUMER / ADAPTER_RANK
    everyone = ("tensor", "dp")

    def spread(block):
        return lax.all_gather(block, everyone, axis=0, tiled=True)

    width = layer_input_rows.shape[1]
    rows = layer_input_rows.shape[0]

    def columns(block):
        full = spread(block)
        groups = full.shape[0] // width
        return full.reshape(groups, width, block.shape[1]).transpose(1, 0, 2).reshape(width, -1)

    full_query = columns(query_weight)
    full_key = columns(key_weight)
    full_value = columns(value_weight)
    full_out_t = columns(output_weight.T)
    full_up = columns(up_weight)
    full_down_t = columns(down_weight.T)
    query_bias = lax.all_gather(query_bias_vector, "tensor", axis=0, tiled=True)
    value_bias = lax.all_gather(value_bias_vector, "tensor", axis=0, tiled=True)
    up_bias = lax.all_gather(up_bias_vector, "tensor", axis=0, tiled=True)
    query_up = lax.all_gather(query_up_trained, "tensor", axis=1, tiled=True)
    value_up = lax.all_gather(value_up_trained, "tensor", axis=1, tiled=True)
    place = lax.axis_index("tensor")
    segment_ids = lax.dynamic_slice_in_dim(segments, place * rows, rows).reshape(-1, SEQ)
    live = lax.dynamic_slice_in_dim(sentence_row_mask, place * rows, rows).reshape(-1, SEQ)
    seqs = rows // SEQ
    heads = width // HEAD_DIM
    x = layer_input_rows
    u_q = mm(x, query_down_frozen).astype(NARROW)
    u_v = mm(x, value_down_frozen).astype(NARROW)
    q = (mm(x, full_query) + query_bias + adapter_scale * mm(u_q, query_up)).astype(NARROW)
    k = mm(x, full_key).astype(NARROW)
    v = (mm(x, full_value) + value_bias + adapter_scale * mm(u_v, value_up)).astype(NARROW)

    def by_heads(block):
        return block.reshape(seqs, SEQ, heads, HEAD_DIM)

    scale = HEAD_DIM ** (-0.5)
    qh, kh, vh = (by_heads(q), by_heads(k), by_heads(v))
    places = jnp.arange(SEQ)
    allowed = (segment_ids[:, :, None] == segment_ids[:, None, :]) & (live[:, None, :] == 1)
    allowed = allowed | (places[:, None] == places[None, :])[None]
    scores = jnp.einsum("sqhd,skhd->shqk", qh, kh, preferred_element_type=WIDE) * scale
    scores = jnp.where(allowed[:, None], scores, NEG_FILL)
    highest = jnp.max(scores, axis=-1, keepdims=True)
    powers = jnp.exp(scores - highest)
    probs = (powers / jnp.sum(powers, axis=-1, keepdims=True)).astype(NARROW)
    context = (
        jnp.einsum("shqk,skhd->sqhd", probs, vh, preferred_element_type=WIDE)
        .astype(NARROW)
        .reshape(rows, width)
    )
    attn = mm_nt(context, full_out_t) + output_bias_vector
    first, n1, s1 = layer_norm(x.astype(WIDE) + attn, first_norm_gain, first_norm_bias)
    middle = first.astype(NARROW)
    inner = mm(middle, full_up) + up_bias
    active, slope = jax.vjp(lambda value: jax.nn.gelu(value, approximate=False), inner)
    ffn = mm_nt(active.astype(NARROW), full_down_t) + down_bias_vector
    output, n2, s2 = layer_norm(first + ffn, second_norm_gain, second_norm_bias)
    grad_second = norm_back(output_gradient.astype(WIDE), n2, s2, second_norm_gain)
    grad_active = mm(grad_second.astype(NARROW), full_down_t)
    grad_inner = slope(grad_active)[0].astype(NARROW)
    grad_first = norm_back(grad_second + mm_nt(grad_inner, full_up), n1, s1, first_norm_gain)
    grad_context = by_heads(mm(grad_first.astype(NARROW), full_out_t).astype(NARROW))
    grad_probs = jnp.einsum("sqhd,skhd->shqk", grad_context, vh, preferred_element_type=WIDE)
    probs_wide = probs.astype(WIDE)
    inside = jnp.sum(probs_wide * grad_probs, axis=-1, keepdims=True)
    grad_scores = (probs_wide * (grad_probs - inside)).astype(NARROW)
    gq = jnp.einsum("shqk,skhd->sqhd", grad_scores, kh, preferred_element_type=WIDE) * scale
    gk = jnp.einsum("shqk,sqhd->skhd", grad_scores, qh, preferred_element_type=WIDE) * scale
    gv = jnp.einsum("shqk,sqhd->skhd", probs, grad_context, preferred_element_type=WIDE)
    gq, gk, gv = (item.astype(NARROW).reshape(rows, width) for item in (gq, gk, gv))
    back_q = adapter_scale * mm_nt(gq, query_up)
    back_v = adapter_scale * mm_nt(gv, value_up)
    grad_input = (
        grad_first
        + mm_nt(gq, full_query)
        + mm_nt(gk, full_key)
        + mm_nt(gv, full_value)
        + mm_nt(back_q, query_down_frozen.astype(WIDE))
        + mm_nt(back_v, value_down_frozen.astype(WIDE))
    )
    grads = jnp.concatenate([mm_tn(u_q, gq), mm_tn(u_v, gv)], axis=0) * adapter_scale
    grads = lax.psum(grads, everyone)
    mine = query_up_trained.shape[1]
    grads = lax.dynamic_slice_in_dim(grads, place * mine, mine, axis=1)
    return (
        output.astype(NARROW),
        grad_input.astype(NARROW),
        grads[:ADAPTER_RANK],
        grads[ADAPTER_RANK:],
    )


IN_SPECS = (
    P(("dp", "tensor"), None),
    P(("dp", "tensor"), None),
    P("dp", "tensor"),
    P("dp", "tensor"),
    P("dp", "tensor"),
    P("tensor", "dp"),
    P("dp", "tensor"),
    P("tensor", "dp"),
    P("tensor"),
    P("tensor"),
    P(),
    P("tensor"),
    P(),
    P(),
    P(),
    P(None, "tensor"),
    P(None, "tensor"),
    P(),
    P(),
    P(),
    P(),
    P("dp"),
    P("dp"),
)
OUT_SPECS = (
    P(("dp", "tensor"), None),
    P(("dp", "tensor"), None),
    P(None, "tensor"),
    P(None, "tensor"),
)


def solution(mesh):
    return jax.shard_map(body, mesh=mesh, in_specs=IN_SPECS, out_specs=OUT_SPECS, check_vma=False)
```

profile of v0, /device:TPU:0, one launch (start us, length us, event | category | flops | bytes accessed | tf_op | source)
XLA Modules:
  0.0 609.4 jit_solution(543538263132884549)
XLA Ops:
  12.2 2.6 copy.141
  16.2 6.2 %all-gather.1 = bf16[4,192,8]{1,2,0:T(8,128)(2,1)S(1)} all-gather(bf16[1,192,8]{1,2,0:T(8,128)(2,1)S(1)} %bitcast.150), channel_id=1, replica_groups=mesh['dp'=8,'tensor'=4] {'tensor'}, dimensions={0}, use_global_device_ids=true | all-gather | bytes 15360 | tf_op jit(solution)/shard_map/all_gather | solution.py:91
  22.5 5.4 all-gather
  31.4 7.4 %all-reduce.2 = (f32[768]{0:T(1024)S(1)}, f32[768]{0:T(1024)S(1)}) all-reduce(f32[768]{0:T(1024)S(1)} %dynamic-update-slice.1, f32[768]{0:T(1024)S(1)} %dynamic-update-slice), channel_id=1, replica_groups=mesh['dp'=8,'tensor'=4] {'tensor'}, use_global_device_ids=true, to_apply=%add.1 | all-reduce | flops 1536 | bytes 12288
  38.8 5.2 all-gather.2
  46.4 22.4 %all-gather.14.cloned.1.call-done = bf16[3072,192]{1,0:T(8,128)(2,1)} async-done(((bf16[96,192]{1,0:T(8,128)(2,1)}), bf16[3072,192]{1,0:T(8,128)(2,1)}) %all-gather.14.cloned.1.call-update) | async-done | bytes 1179664 | tf_op jit(solution)/shard_map/all_gather | solution.py:72
  68.8 2.7 copy.172
  75.8 2.9 reshape.154
  78.7 47.1 %all-gather.12.cloned.1.call-done = bf16[3072,192]{1,0:T(8,128)(2,1)} async-done(((bf16[96,192]{1,0:T(8,128)(2,1)}), bf16[3072,192]{1,0:T(8,128)(2,1)}) %all-gather.12.cloned.1.call-update) | async-done | bytes 1179664 | tf_op jit(solution)/shard_map/all_gather | solution.py:72
  125.7 3.6 copy.171
  133.9 2.6 copy.127
  136.5 3.8 reshape.151
  140.4 42.3 %all-gather.10.cloned.1.call-done = bf16[3072,192]{1,0:T(8,128)(2,1)} async-done(((bf16[96,192]{1,0:T(8,128)(2,1)}), bf16[3072,192]{1,0:T(8,128)(2,1)}) %all-gather.10.cloned.1.call-update) | async-done | bytes 1179664 | tf_op jit(solution)/shard_map/all_gather | solution.py:72
  182.7 3.6 copy.170
  191.4 2.9 reshape.148
  194.4 14.7 %fusion.69 = (f32[2,12,512]{2,1,0:T(8,128)S(1)}, f32[2,12,512,512]{2,3,1,0:T(8,128)}) fusion(pred[2,512,512]{1,2,0:T(8,128)(4,1)} %and_or_fusion, bf16[2,512,12,64]{1,0,3,2:T(2,128)(2,1)S(1)} %reshape.154, bf16[2,512,12,64]{1,0,3,2:T(2,128)(2,1)} %reshape.151), kind=kOutput, calls=%fused_computation.113 | convolution fusion | flops 830472704 | bytes 28884992 | tf_op jit(solution)/shard_map/sub | solution.py:116
  209.1 10.2 %divide_convert_fusion = bf16[2,12,512,512]{2,3,1,0:T(8,128)(2,1)S(1)} fusion(f32[2,12,512,512]{2,3,1,0:T(8,128)} %get-tuple-element.30, f32[2,12,512]{2,1,0:T(8,128)S(1)} %get-tuple-element.29), kind=kLoop, calls=%fused_computation.5 | loop fusion | flops 12582912 | bytes 37797888 | tf_op jit(solution)/shard_map/convert_element_type | solution.py:117
  219.3 2.0 fusion.30
  221.3 2.5 copy-done.1
  227.0 12.4 %all-gather.16.cloned.1.call-done = bf16[3072,192]{1,0:T(8,128)(2,1)} async-done(((bf16[96,192]{1,0:T(8,128)(2,1)}), bf16[3072,192]{1,0:T(8,128)(2,1)}) %all-gather.16.cloned.1.call-update) | async-done | bytes 1179664 | tf_op jit(solution)/shard_map/all_gather | solution.py:72
  239.4 2.7 copy.173
  242.3 4.0 fusion.78
  246.7 58.1 %all-gather.20.cloned.1.call-done = bf16[3072,768]{1,0:T(8,128)(2,1)} async-done(((bf16[96,768]{1,0:T(8,128)(2,1)}), bf16[3072,768]{1,0:T(8,128)(2,1)}) %all-gather.20.cloned.1.call-update) | async-done | bytes 4718608 | tf_op jit(solution)/shard_map/all_gather | solution.py:72
  304.8 6.7 %copy.140 = bf16[768,4,768]{0,2,1:T(8,128)(2,1)} copy(bf16[768,4,768]{2,0,1:T(8,128)(2,1)} %bitcast.121) | data formatting | bytes 9437184 | tf_op jit(solution)/shard_map/transpose | solution.py:80
  311.4 58.6 %all-gather.18.cloned.1.call-done = bf16[3072,768]{1,0:T(8,128)(2,1)} async-done(((bf16[96,768]{1,0:T(8,128)(2,1)}), bf16[3072,768]{1,0:T(8,128)(2,1)}) %all-gather.18.cloned.1.call-update) | async-done | bytes 4718608 | tf_op jit(solution)/shard_map/all_gather | solution.py:72
  370.0 6.7 %copy.139 = bf16[768,4,768]{0,2,1:T(8,128)(2,1)} copy(bf16[768,4,768]{2,0,1:T(8,128)(2,1)} %bitcast.122) | data formatting | bytes 9437184 | tf_op jit(solution)/shard_map/transpose | solution.py:80
  376.7 36.2 %fusion.4 = (f32[1024,3072]{1,0:T(8,128)}, f32[1024,3072]{1,0:T(8,128)}) fusion(f32[3072]{0:T(1024)S(1)} %bitcast.147, bf16[768,3072]{0,1:T(8,128)(2,1)} %bitcast.125, f32[1024,768]{0,1:T(8,128)S(1)} %get-tuple-element.32, f32[768]{0:T(1024)S(1)} %copy-done.38, f32[768]{0:T(1024)S(1)} %copy-done.39, f32[1024]{0:T(1024)S(1)} %add_rsqrt_fusion.1, ...), kind=kOutput, calls=%fused_computation.10 | convolution fusion | flops 5033951232 | bytes 33056768 | tf_op jit(solution)/shard_map/dot_general | solution.py:32
  413.0 17.1 %fusion.79 = (f32[1024]{0:T(1024)S(1)}, f32[1024,768]{0,1:T(8,128)}) fusion(f32[768]{0:T(1024)S(1)} %copy-done.37, bf16[768,3072]{0,1:T(8,128)(2,1)} %bitcast.123, f32[1024,3072]{1,0:T(8,128)} %get-tuple-element.33, f32[1024,3072]{1,0:T(8,128)} %get-tuple-element.34, f32[3072]{0:T(1024)S(1)} %bitcast.148, f32[768]{0:T(1024)S(1)} %copy-done.38, ...), kind=kOutput, calls=%fused_computation.115 | convolution fusion | flops 4849925120 | bytes 36209664 | tf_op jit(solution)/shard_map/dot_general | solution.py:36
  430.1 2.4 multiply_reduce_fusion.2
  432.9 3.7 fusion.19
  436.6 25.4 %fusion.67 = (f32[1024]{0:T(1024)S(1)}, f32[1024]{0:T(1024)S(1)}, f32[1024,768]{0,1:T(8,128)}) fusion(f32[1024]{0:T(1024)S(1)} %add_rsqrt_fusion.1, f32[1024,768]{0,1:T(8,128)S(1)} %get-tuple-element.32, f32[1024]{0:T(1024)S(1)} %broadcast_multiply_fusion.5, f32[768]{0:T(1024)S(1)} %copy-done.39, bf16[768,3072]{0,1:T(8,128)(2,1)} %bitcast.126, ...), kind=kOutput, calls=%fused_computation.111 | convolution fusion | flops 9729734656 | bytes 45664256 | tf_op jit(solution)/shard_map/dot_general | solution.py:36
  462.0 5.5 convolution_convert_fusion.2
  467.5 2.8 copy.142
  470.3 2.9 reshape.162
  473.2 12.9 %fusion.1 = (f32[2,12,512]{2,1,0:T(8,128)S(1)}, f32[2,12,512,512]{2,3,1,0:T(8,128)}) fusion(bf16[2,12,512,512]{2,3,1,0:T(8,128)(2,1)} %copy-done.1, bf16[2,512,12,64]{1,0,3,2:T(2,128)(2,1)S(1)} %copy-done.4, bf16[2,512,12,64]{1,0,3,2:T(2,128)(2,1)S(1)} %reshape.162), kind=kOutput, calls=%fused_computation.3 | convolution fusion | flops 824168448 | bytes 40943616 | tf_op jit(solution)/shard_map/sqhd,skhd->shqk/dot_general | solution.py:135
  486.1 8.5 %fusion.31 = bf16[2,512,12,64]{1,3,2,0:T(8,128)(2,1)S(1)} fusion(bf16[2,12,512,512]{2,3,1,0:T(8,128)(2,1)} %copy-done.1, bf16[2,512,12,64]{1,0,3,2:T(2,128)(2,1)S(1)} %reshape.162), kind=kOutput, calls=%fused_computation.69 | convolution fusion | flops 806092800 | bytes 15728640 | tf_op jit(solution)/shard_map/shqk,sqhd->skhd/dot_general | solution.py:141
  494.6 17.1 %fusion.2 = bf16[2,12,512,512]{2,3,1,0:T(8,128)(2,1)S(1)} fusion(f32[2,12,512,512]{2,3,1,0:T(8,128)} %get-tuple-element.39, f32[2,12,512]{2,1,0:T(8,128)S(1)} %get-tuple-element.38, f32[2,12,512,512]{2,3,1,0:T(8,128)} %get-tuple-element.30, f32[2,12,512]{2,1,0:T(8,128)S(1)} %copy-done.18), kind=kLoop, calls=%fused_computation.4 | loop fusion | flops 37748736 | bytes 63012864 | tf_op jit(solution)/shard_map/convert_element_type | solution.py:138
  511.7 4.5 copy-done.2
  516.2 2.1 fusion.32
  518.3 9.6 %fusion.33 = bf16[2,512,12,64]{1,3,2,0:T(8,128)(2,1)} fusion(bf16[2,12,512,512]{2,3,1,0:T(8,128)(2,1)} %copy-done.2, bf16[2,512,12,64]{1,0,3,2:T(2,128)(2,1)S(1)} %copy-done.10), kind=kOutput, calls=%fused_computation.71 | convolution fusion | flops 806879232 | bytes 15728640 | tf_op jit(solution)/shard_map/shqk,sqhd->skhd/dot_general | solution.py:140
  530.0 2.5 fusion.52
  532.5 4.4 fusion.84
  538.9 3.2 fusion.86
  543.1 2.8 copy.159
  545.9 3.1 copy.151
  549.5 3.1 fusion.85
  552.6 7.4 %add_convert_fusion.2 = bf16[1024,768]{0,1:T(8,128)(2,1)S(1)} fusion(f32[1024,768]{0,1:T(8,128)} %fusion.52, f32[1024,768]{0,1:T(8,128)} %fusion.86, f32[1024,768]{0,1:T(8,128)} %fusion.85, f32[1024,768]{0,1:T(8,128)} %fusion.84, bf16[768,8]{0,1:T(8,128)(2,1)S(1)} %copy-done.28, bf16[1024,768]{0,1:T(8,128)(2,1)S(1)} %bitcast.113, ...), kind=kOutput, calls=%fused_computation.34 | convolution fusion | flops 34611200 | bytes 22061056 | tf_op jit(solution)/shard_map/dot_general | solution.py:36
  561.7 40.0 %psum.7 = f32[16,768]{1,0:T(8,128)S(1)} all-reduce(f32[16,768]{1,0:T(8,128)S(1)} %maximum_multiply_fusion), channel_id=1, replica_groups=mesh['dp'=8,'tensor'=4] {'tensor','dp'}, use_global_device_ids=true, to_apply=%region_11.12 | all-reduce | flops 12288 | bytes 98304 | tf_op jit(solution)/shard_map/psum | solution.py:154
  (143 shorter events, 37.6 us)
Async XLA Ops:
  7.2 38.2 %copy-start = (bf16[768,8]{0,1:T(8,128)(2,1)S(1)}, bf16[768,8]{0,1:T(8,128)(2,1)}, u32[]{:S(2)}) copy-start(bf16[768,8]{0,1:T(8,128)(2,1)} %param.36) | copy-start | bytes 36868
  7.2 7.6 %copy-start.33 = (f32[768]{0:T(1024)S(1)}, f32[768]{0:T(1024)}, u32[]{:S(2)}) copy-start(f32[768]{0:T(1024)} %param.34) | copy-start | bytes 9220
  7.2 9.0 %copy-start.31 = (bf16[8,192]{1,0:T(8,128)(2,1)S(1)}, bf16[8,192]{1,0:T(8,128)(2,1)}, u32[]{:S(2)}) copy-start(bf16[8,192]{1,0:T(8,128)(2,1)} %param.38) | copy-start | bytes 9220
  7.2 15.3 %copy-start.32 = (bf16[8,192]{1,0:T(8,128)(2,1)S(1)}, bf16[8,192]{1,0:T(8,128)(2,1)}, u32[]{:S(2)}) copy-start(bf16[8,192]{1,0:T(8,128)(2,1)} %param.39) | copy-start | bytes 9220
  7.2 20.8 %copy-start.5 = (bf16[1024,768]{1,0:T(8,128)(2,1)S(1)}, bf16[1024,768]{1,0:T(8,128)(2,1)}, u32[]{:S(2)}) copy-start(bf16[1024,768]{1,0:T(8,128)(2,1)} %param.23) | copy-start | bytes 4718596
  7.2 61.6 %all-gather.14.cloned.1.call-start = ((), (), s32[]{:S(2)}) async-start(), calls=%async_computation.2 | async-start | bytes 1622016 | tf_op jit(solution)/shard_map/all_gather | solution.py:72
  8.0 117.8 %all-gather.12.cloned.1.call-start = ((), (), s32[]{:S(2)}) async-start(), calls=%async_computation.1 | async-start | bytes 1622016 | tf_op jit(solution)/shard_map/all_gather | solution.py:72
  8.7 173.9 %all-gather.10.cloned.1.call-start = ((), (), s32[]{:S(2)}) async-start(), calls=%async_computation | async-start | bytes 1622016 | tf_op jit(solution)/shard_map/all_gather | solution.py:72
  9.4 230.0 %all-gather.16.cloned.1.call-start = ((), (), s32[]{:S(2)}) async-start(), calls=%async_computation.3 | async-start | bytes 1622016 | tf_op jit(solution)/shard_map/all_gather | solution.py:72
  11.0 293.8 %all-gather.20.cloned.1.call-start = ((), (), s32[]{:S(2)}) async-start(), calls=%async_computation.5 | async-start | bytes 4866048 | tf_op jit(solution)/shard_map/all_gather | solution.py:72
  11.6 358.4 %all-gather.18.cloned.1.call-start = ((), (), s32[]{:S(2)}) async-start(), calls=%async_computation.4 | async-start | bytes 4866048 | tf_op jit(solution)/shard_map/all_gather | solution.py:72
  12.2 17.5 %copy-start.40 = (u32[32]{0:T(128)S(1)}, u32[32]{0:T(128)}, u32[]{:S(2)}) copy-start(u32[32]{0:T(128)} %constant.103) | copy-start | bytes 388
  12.2 18.7 %copy-start.34 = (f32[192]{0:T(256)S(1)}, f32[192]{0:T(256)}, u32[]{:S(2)}) copy-start(f32[192]{0:T(256)} %param.31) | copy-start | bytes 2308
  12.2 18.9 %copy-start.35 = (f32[192]{0:T(256)S(1)}, f32[192]{0:T(256)}, u32[]{:S(2)}) copy-start(f32[192]{0:T(256)} %param.32) | copy-start | bytes 2308
  14.8 31.1 %copy-start.27 = (bf16[768,8]{0,1:T(8,128)(2,1)S(1)}, bf16[768,8]{0,1:T(8,128)(2,1)}, u32[]{:S(2)}) copy-start(bf16[768,8]{0,1:T(8,128)(2,1)} %param.37) | copy-start | bytes 36868
  22.5 109.6 %copy-start.25 = (bf16[768,8]{0,1:T(8,128)(2,1)}, bf16[768,8]{0,1:T(8,128)(2,1)S(1)}, u32[]{:S(2)}) copy-start(bf16[768,8]{0,1:T(8,128)(2,1)S(1)} %reshape.175) | copy-start | bytes 36868
  28.0 161.1 %copy-start.23 = (bf16[768,8]{0,1:T(8,128)(2,1)}, bf16[768,8]{0,1:T(8,128)(2,1)S(1)}, u32[]{:S(2)}) copy-start(bf16[768,8]{0,1:T(8,128)(2,1)S(1)} %reshape.173) | copy-start | bytes 36868
  45.9 86.3 %copy-start.19 = (bf16[1024,8]{0,1:T(8,128)(2,1)}, bf16[1024,8]{0,1:T(8,128)(2,1)S(1)}, u32[]{:S(2)}) copy-start(bf16[1024,8]{0,1:T(8,128)(2,1)S(1)} %convolution_convert_fusion.4) | copy-start | bytes 49156
  46.4 142.7 %copy-start.21 = (bf16[1024,8]{0,1:T(8,128)(2,1)}, bf16[1024,8]{0,1:T(8,128)(2,1)S(1)}, u32[]{:S(2)}) copy-start(bf16[1024,8]{0,1:T(8,128)(2,1)S(1)} %convolution_convert_fusion.5) | copy-start | bytes 49156
  71.7 1.0 copy-start.11
  78.6 115.7 %copy-start.8 = (bf16[2,512,12,64]{1,0,3,2:T(2,128)(2,1)}, bf16[2,512,12,64]{1,0,3,2:T(2,128)(2,1)S(1)}, u32[]{:S(2)}) copy-start(bf16[2,512,12,64]{1,0,3,2:T(2,128)(2,1)S(1)} %reshape.154) | copy-start | bytes 4718596
  130.7 1.4 copy-start.13
  187.6 1.4 copy-start.14
  194.3 25.0 %copy-start.3 = (bf16[2,512,12,64]{1,0,3,2:T(2,128)(2,1)}, bf16[2,512,12,64]{1,0,3,2:T(2,128)(2,1)S(1)}, u32[]{:S(2)}) copy-start(bf16[2,512,12,64]{1,0,3,2:T(2,128)(2,1)S(1)} %reshape.148) | copy-start | bytes 4718596
  209.1 10.2 %copy-start.17 = (f32[2,12,512]{2,1,0:T(8,128)}, f32[2,12,512]{2,1,0:T(8,128)S(1)}, u32[]{:S(2)}) copy-start(f32[2,12,512]{2,1,0:T(8,128)S(1)} %get-tuple-element.29) | copy-start | bytes 147460
  219.3 4.5 copy-start.1
  227.0 15.3 %copy-start.36 = (f32[768]{0:T(1024)S(1)}, f32[768]{0:T(1024)}, u32[]{:S(2)}) copy-start(f32[768]{0:T(1024)} %param.33) | copy-start | bytes 9220
  242.3 4.0 copy-start.16
  246.3 215.7 %copy-start.6 = (f32[1024,768]{0,1:T(8,128)}, f32[1024,768]{0,1:T(8,128)S(1)}, u32[]{:S(2)}) copy-start(f32[1024,768]{0,1:T(8,128)S(1)} %get-tuple-element.32) | copy-start | bytes 9437188
  370.0 6.7 %copy-start.38 = (f32[768]{0:T(1024)S(1)}, f32[768]{0:T(1024)}, u32[]{:S(2)}) copy-start(f32[768]{0:T(1024)} %param.41) | copy-start | bytes 9220
  370.0 6.7 %copy-start.39 = (f32[768]{0:T(1024)S(1)}, f32[768]{0:T(1024)}, u32[]{:S(2)}) copy-start(f32[768]{0:T(1024)} %param.40) | copy-start | bytes 9220
  376.7 36.2 %copy-start.37 = (f32[768]{0:T(1024)S(1)}, f32[768]{0:T(1024)}, u32[]{:S(2)}) copy-start(f32[768]{0:T(1024)} %param.35) | copy-start | bytes 9220
  430.1 2.8 copy-start.7
  430.1 2.8 copy-start.29
  430.1 2.8 copy-start.30
  467.5 5.7 copy-start.4
  486.1 8.5 %copy-start.18 = (f32[2,12,512]{2,1,0:T(8,128)S(1)}, f32[2,12,512]{2,1,0:T(8,128)}, u32[]{:S(2)}) copy-start(f32[2,12,512]{2,1,0:T(8,128)} %copy-done.17) | copy-start | bytes 147460
  494.6 21.6 %copy-start.9 = (bf16[2,512,12,64]{1,0,3,2:T(2,128)(2,1)S(1)}, bf16[2,512,12,64]{1,0,3,2:T(2,128)(2,1)}, u32[]{:S(2)}) copy-start(bf16[2,512,12,64]{1,0,3,2:T(2,128)(2,1)} %copy-done.8) | copy-start | bytes 4718596
  511.7 4.5 copy-start.2
  516.2 2.1 copy-start.10
  528.0 2.0 copy-start.26
  536.9 2.0 copy-start.15
  538.9 3.2 copy-start.22
  538.9 3.7 copy-start.20
  545.9 3.5 copy-start.12
  549.5 3.2 copy-start.24
  549.5 3.2 copy-start.28
Sparse Core Ops, SparseCore 0:
  11.0 57.8 all-gather.13
  71.7 53.9 all-gather.11
  128.6 53.9 all-gather.9
  185.4 53.9 all-gather.15
  242.2 62.5 all-gather.19
  307.5 62.4 all-gather.17
where the time goes:
time: 619 us; the launch traced here: 609 us
  waiting for transfers between devices  244 us (39%)
  matrix products  167 us (27%)
  local copies, waits for them, and re-layouts  82.2 us (13%)
  blocking collectives  64.1 us (10%)
  other arithmetic  35.9 us (6%)
  between operations  15.6 us (3%)
    all_gather x6, waiting for transfers between devices, spread(): return lax.all_gather(block, everyone, axis=0, tiled=True)  241 us
    dot_general x8, matrix products, mm_nt(): lax.dot_general(left, right, (((1,), (1,)), ((), ())), preferred_element_...  67 us
    dot_general x9, matrix products, mm(): return jnp.dot(left, right, preferred_element_type=WIDE)  49.5 us
    psum x1, blocking collectives, body(): grads = lax.psum(grads, everyone)  40 us
    unnamed x99, local copies, waits for them, and re-layouts  22.7 us
    convert_element_type x1, other arithmetic, body(): grad_scores = (probs_wide * (grad_probs - inside)).astype(NARROW)  17.1 us
    transpose x6, local copies, waits for them, and re-layouts, columns(): full.reshape(groups, width, block.shape[1]).transpose(1, 0, 2)  16.4 us
    sub x1, matrix products, body(): powers = jnp.exp(scores - highest)  14.7 us
  transfers between devices with their start and end apart: 6, of which 6 were waited for; matrix products, arithmetic and copies ran while one was open for 15% of the time, Pallas kernels for 0%

commit v1 on v0

--- a/solution.py
+++ b/solution.py
@@ -151,7 +151,7 @@
         + mm_nt(back_v, value_down_frozen.astype(WIDE))
     )
     grads = jnp.concatenate([mm_tn(u_q, gq), mm_tn(u_v, gv)], axis=0) * adapter_scale
-    grads = lax.psum(grads, everyone)
+    grads = jnp.sum(lax.all_gather(grads, everyone), axis=0)
     mine = query_up_trained.shape[1]
     grads = lax.dynamic_slice_in_dim(grads, place * mine, mine, axis=1)
     return (

time: 619 us -> 597 us (0.964)
  blocking collectives: 64.1 us -> 24.1 us
  waiting for transfers between devices: 244 us -> 263 us
    psum x1 -> x0, blocking collectives: 40 us -> none  [body(): grads = lax.psum(grads, everyone)]
    all_gather x0 -> x1, waiting for transfers between devices: none -> 19.3 us  [body(): grads = jnp.sum(lax.all_gather(grads, everyone), axis=0)]
    unnamed x99 -> x103, local copies, waits for them, and re-layouts: 22.7 us -> 20.5 us
  transfers between devices with their start and end apart: 6 -> 7, of which waited for: 6 -> 7; matrix products, arithmetic and copies ran while one was open for 15% -> 21% of each run, Pallas kernels for 0% -> 0%
where the time goes in v1:
time: 597 us; the launch traced here: 588 us
  waiting for transfers between devices  263 us (44%)
  matrix products  168 us (28%)
  local copies, waits for them, and re-layouts  78.5 us (13%)
  other arithmetic  38 us (6%)
  blocking collectives  24.1 us (4%)
  between operations  15.6 us (3%)
    all_gather x6, waiting for transfers between devices, spread(): return lax.all_gather(block, everyone, axis=0, tiled=True)  241 us
    dot_general x8, matrix products, mm_nt(): lax.dot_general(left, right, (((1,), (1,)), ((), ())), preferred_element_...  67.4 us
    dot_general x9, matrix products, mm(): return jnp.dot(left, right, preferred_element_type=WIDE)  49.5 us
    unnamed x103, local copies, waits for them, and re-layouts  20.5 us
    all_gather x1, waiting for transfers between devices, body(): grads = jnp.sum(lax.all_gather(grads, everyone), axis=0)  19.3 us
    convert_element_type x1, other arithmetic, body(): grad_scores = (probs_wide * (grad_probs - inside)).astype(NARROW)  17.1 us
    transpose x6, local copies, waits for them, and re-layouts, columns(): full.reshape(groups, width, block.shape[1]).transpose(1, 0, 2)  16.3 us
    sub x1, matrix products, body(): powers = jnp.exp(scores - highest)  14.7 us
  transfers between devices with their start and end apart: 7, of which 7 were waited for; matrix products, arithmetic and copies ran while one was open for 21% of the time, Pallas kernels for 0%

profile of v1, /device:TPU:0, one launch (start us, length us, event | category | flops | bytes accessed | tf_op | source)
XLA Modules:
  0.0 588.1 jit_solution(11366298508995397647)
XLA Ops:
  12.3 2.6 copy.141
  16.3 6.2 %all-gather.1 = bf16[4,192,8]{1,2,0:T(8,128)(2,1)S(1)} all-gather(bf16[1,192,8]{1,2,0:T(8,128)(2,1)S(1)} %bitcast.154), channel_id=1, replica_groups=mesh['dp'=8,'tensor'=4] {'tensor'}, dimensions={0}, use_global_device_ids=true | all-gather | bytes 15360 | tf_op jit(solution)/shard_map/all_gather | solution.py:91
  22.6 5.4 all-gather
  28.1 1.6 copy.119
  31.4 7.4 %all-reduce.2 = (f32[768]{0:T(1024)S(1)}, f32[768]{0:T(1024)S(1)}) all-reduce(f32[768]{0:T(1024)S(1)} %dynamic-update-slice.1, f32[768]{0:T(1024)S(1)} %dynamic-update-slice), channel_id=1, replica_groups=mesh['dp'=8,'tensor'=4] {'tensor'}, use_global_device_ids=true, to_apply=%add.1 | all-reduce | flops 1536 | bytes 12288
  38.8 5.2 all-gather.2
  46.4 22.4 %all-gather.15.cloned.1.call-done = bf16[3072,192]{1,0:T(8,128)(2,1)} async-done(((bf16[96,192]{1,0:T(8,128)(2,1)}), bf16[3072,192]{1,0:T(8,128)(2,1)}) %all-gather.15.cloned.1.call-update) | async-done | bytes 1179664 | tf_op jit(solution)/shard_map/all_gather | solution.py:72
  68.8 2.7 copy.172
  75.8 2.9 reshape.183
  78.7 47.1 %all-gather.13.cloned.1.call-done = bf16[3072,192]{1,0:T(8,128)(2,1)} async-done(((bf16[96,192]{1,0:T(8,128)(2,1)}), bf16[3072,192]{1,0:T(8,128)(2,1)}) %all-gather.13.cloned.1.call-update) | async-done | bytes 1179664 | tf_op jit(solution)/shard_map/all_gather | solution.py:72
  125.7 3.6 copy.171
  132.2 1.8 add_convert_fusion.4
  134.0 2.6 copy.127
  136.5 3.9 reshape.180
  140.4 42.2 %all-gather.11.cloned.1.call-done = bf16[3072,192]{1,0:T(8,128)(2,1)} async-done(((bf16[96,192]{1,0:T(8,128)(2,1)}), bf16[3072,192]{1,0:T(8,128)(2,1)}) %all-gather.11.cloned.1.call-update) | async-done | bytes 1179664 | tf_op jit(solution)/shard_map/all_gather | solution.py:72
  182.7 3.6 copy.170
  191.4 2.9 reshape.177
  194.3 14.7 %fusion.69 = (f32[2,12,512]{2,1,0:T(8,128)S(1)}, f32[2,12,512,512]{2,3,1,0:T(8,128)}) fusion(pred[2,512,512]{1,2,0:T(8,128)(4,1)} %and_or_fusion, bf16[2,512,12,64]{1,0,3,2:T(2,128)(2,1)S(1)} %reshape.183, bf16[2,512,12,64]{1,0,3,2:T(2,128)(2,1)} %reshape.180), kind=kOutput, calls=%fused_computation.115 | convolution fusion | flops 830472704 | bytes 28884992 | tf_op jit(solution)/shard_map/sub | solution.py:116
  209.0 10.2 %divide_convert_fusion = bf16[2,12,512,512]{2,3,1,0:T(8,128)(2,1)S(1)} fusion(f32[2,12,512,512]{2,3,1,0:T(8,128)} %get-tuple-element.30, f32[2,12,512]{2,1,0:T(8,128)S(1)} %get-tuple-element.29), kind=kLoop, calls=%fused_computation.5 | loop fusion | flops 12582912 | bytes 37797888 | tf_op jit(solution)/shard_map/convert_element_type | solution.py:117
  219.2 2.0 fusion.30
  221.2 2.5 copy-done.1
  226.9 12.5 %all-gather.17.cloned.1.call-done = bf16[3072,192]{1,0:T(8,128)(2,1)} async-done(((bf16[96,192]{1,0:T(8,128)(2,1)}), bf16[3072,192]{1,0:T(8,128)(2,1)}) %all-gather.17.cloned.1.call-update) | async-done | bytes 1179664 | tf_op jit(solution)/shard_map/all_gather | solution.py:72
  239.4 2.7 copy.173
  242.3 4.0 fusion.78
  246.7 58.1 %all-gather.21.cloned.1.call-done = bf16[3072,768]{1,0:T(8,128)(2,1)} async-done(((bf16[96,768]{1,0:T(8,128)(2,1)}), bf16[3072,768]{1,0:T(8,128)(2,1)}) %all-gather.21.cloned.1.call-update) | async-done | bytes 4718608 | tf_op jit(solution)/shard_map/all_gather | solution.py:72
  304.8 6.7 %copy.140 = bf16[768,4,768]{0,2,1:T(8,128)(2,1)} copy(bf16[768,4,768]{2,0,1:T(8,128)(2,1)} %bitcast.125) | data formatting | bytes 9437184 | tf_op jit(solution)/shard_map/transpose | solution.py:80
  311.4 58.6 %all-gather.19.cloned.1.call-done = bf16[3072,768]{1,0:T(8,128)(2,1)} async-done(((bf16[96,768]{1,0:T(8,128)(2,1)}), bf16[3072,768]{1,0:T(8,128)(2,1)}) %all-gather.19.cloned.1.call-update) | async-done | bytes 4718608 | tf_op jit(solution)/shard_map/all_gather | solution.py:72
  370.1 6.6 %copy.139 = bf16[768,4,768]{0,2,1:T(8,128)(2,1)} copy(bf16[768,4,768]{2,0,1:T(8,128)(2,1)} %bitcast.126) | data formatting | bytes 9437184 | tf_op jit(solution)/shard_map/transpose | solution.py:80
  376.7 36.2 %fusion.4 = (f32[1024,3072]{1,0:T(8,128)}, f32[1024,3072]{1,0:T(8,128)}) fusion(f32[3072]{0:T(1024)S(1)} %bitcast.151, bf16[768,3072]{0,1:T(8,128)(2,1)} %bitcast.129, f32[1024,768]{0,1:T(8,128)S(1)} %get-tuple-element.32, f32[768]{0:T(1024)S(1)} %copy-done.40, f32[768]{0:T(1024)S(1)} %copy-done.41, f32[1024]{0:T(1024)S(1)} %add_rsqrt_fusion.1, ...), kind=kOutput, calls=%fused_computation.10 | convolution fusion | flops 5033951232 | bytes 33056768 | tf_op jit(solution)/shard_map/dot_general | solution.py:32
  413.0 17.1 %fusion.79 = (f32[1024]{0:T(1024)S(1)}, f32[1024,768]{0,1:T(8,128)}) fusion(f32[768]{0:T(1024)S(1)} %copy-done.39, bf16[768,3072]{0,1:T(8,128)(2,1)} %bitcast.127, f32[1024,3072]{1,0:T(8,128)} %get-tuple-element.33, f32[1024,3072]{1,0:T(8,128)} %get-tuple-element.34, f32[3072]{0:T(1024)S(1)} %bitcast.152, f32[768]{0:T(1024)S(1)} %copy-done.40, ...), kind=kOutput, calls=%fused_computation.117 | convolution fusion | flops 4849925120 | bytes 36209664 | tf_op jit(solution)/shard_map/dot_general | solution.py:36
  430.0 2.4 multiply_reduce_fusion.2
  432.9 3.6 fusion.19
  436.5 25.4 %fusion.67 = (f32[1024]{0:T(1024)S(1)}, f32[1024]{0:T(1024)S(1)}, f32[1024,768]{0,1:T(8,128)}) fusion(f32[1024]{0:T(1024)S(1)} %add_rsqrt_fusion.1, f32[1024,768]{0,1:T(8,128)S(1)} %get-tuple-element.32, f32[1024]{0:T(1024)S(1)} %broadcast_multiply_fusion.5, f32[768]{0:T(1024)S(1)} %copy-done.41, bf16[768,3072]{0,1:T(8,128)(2,1)} %bitcast.130, ...), kind=kOutput, calls=%fused_computation.113 | convolution fusion | flops 9729734656 | bytes 45664256 | tf_op jit(solution)/shard_map/dot_general | solution.py:36
  461.9 5.5 convolution_convert_fusion.2
  467.5 2.8 copy.142
  470.3 2.9 reshape.191
  473.2 12.9 %fusion.1 = (f32[2,12,512]{2,1,0:T(8,128)S(1)}, f32[2,12,512,512]{2,3,1,0:T(8,128)}) fusion(bf16[2,12,512,512]{2,3,1,0:T(8,128)(2,1)} %copy-done.1, bf16[2,512,12,64]{1,0,3,2:T(2,128)(2,1)S(1)} %copy-done.4, bf16[2,512,12,64]{1,0,3,2:T(2,128)(2,1)S(1)} %reshape.191), kind=kOutput, calls=%fused_computation.3 | convolution fusion | flops 824168448 | bytes 40943616 | tf_op jit(solution)/shard_map/sqhd,skhd->shqk/dot_general | solution.py:135
  486.0 9.7 %fusion.31 = bf16[2,512,12,64]{1,3,2,0:T(8,128)(2,1)} fusion(bf16[2,12,512,512]{2,3,1,0:T(8,128)(2,1)} %copy-done.1, bf16[2,512,12,64]{1,0,3,2:T(2,128)(2,1)S(1)} %reshape.191), kind=kOutput, calls=%fused_computation.69 | convolution fusion | flops 806092800 | bytes 15728640 | tf_op jit(solution)/shard_map/shqk,sqhd->skhd/dot_general | solution.py:141
  497.3 17.1 %fusion.2 = bf16[2,12,512,512]{2,3,1,0:T(8,128)(2,1)S(1)} fusion(f32[2,12,512,512]{2,3,1,0:T(8,128)} %get-tuple-element.39, f32[2,12,512]{2,1,0:T(8,128)S(1)} %get-tuple-element.38, f32[2,12,512,512]{2,3,1,0:T(8,128)} %get-tuple-element.30, f32[2,12,512]{2,1,0:T(8,128)S(1)} %copy-done.20), kind=kLoop, calls=%fused_computation.4 | loop fusion | flops 37748736 | bytes 63012864 | tf_op jit(solution)/shard_map/convert_element_type | solution.py:138
  514.5 2.1 fusion.32
  516.6 2.4 copy-done.2
  524.8 9.0 %fusion.33 = bf16[2,512,12,64]{1,3,2,0:T(8,128)(2,1)S(1)} fusion(bf16[2,12,512,512]{2,3,1,0:T(8,128)(2,1)} %copy-done.2, bf16[2,512,12,64]{1,0,3,2:T(2,128)(2,1)} %reshape.180), kind=kOutput, calls=%fused_computation.71 | convolution fusion | flops 806879232 | bytes 15728640 | tf_op jit(solution)/shard_map/shqk,sqhd->skhd/dot_general | solution.py:140
  537.0 2.5 fusion.52
  539.4 4.7 fusion.86
  544.2 3.2 fusion.84
  547.4 3.1 fusion.85
  550.5 7.4 %add_convert_fusion.2 = bf16[1024,768]{0,1:T(8,128)(2,1)S(1)} fusion(f32[1024,768]{0,1:T(8,128)} %fusion.52, f32[1024,768]{0,1:T(8,128)} %fusion.86, f32[1024,768]{0,1:T(8,128)} %fusion.85, f32[1024,768]{0,1:T(8,128)} %fusion.84, bf16[768,8]{0,1:T(8,128)(2,1)S(1)} %copy-done.30, bf16[1024,768]{0,1:T(8,128)(2,1)S(1)} %bitcast.117, ...), kind=kOutput, calls=%fused_computation.34 | convolution fusion | flops 34611200 | bytes 22061056 | tf_op jit(solution)/shard_map/dot_general | solution.py:36
  559.5 19.3 %all-gather.23.cloned.1.call-done = f32[32,16,768]{2,1,0:T(8,128)} async-done(((f32[1,16,768]{2,1,0:T(8,128)}), f32[32,16,768]{2,1,0:T(8,128)}) %all-gather.23.cloned.1.call-update) | async-done | bytes 1572880 | tf_op jit(solution)/shard_map/all_gather | solution.py:154
  (150 shorter events, 40.6 us)
Async XLA Ops:
  7.2 38.2 %copy-start = (bf16[768,8]{0,1:T(8,128)(2,1)S(1)}, bf16[768,8]{0,1:T(8,128)(2,1)}, u32[]{:S(2)}) copy-start(bf16[768,8]{0,1:T(8,128)(2,1)} %param.36) | copy-start | bytes 36868
  7.2 7.7 %copy-start.35 = (f32[768]{0:T(1024)S(1)}, f32[768]{0:T(1024)}, u32[]{:S(2)}) copy-start(f32[768]{0:T(1024)} %param.34) | copy-start | bytes 9220
  7.2 9.1 %copy-start.33 = (bf16[8,192]{1,0:T(8,128)(2,1)S(1)}, bf16[8,192]{1,0:T(8,128)(2,1)}, u32[]{:S(2)}) copy-start(bf16[8,192]{1,0:T(8,128)(2,1)} %param.38) | copy-start | bytes 9220
  7.2 15.4 %copy-start.34 = (bf16[8,192]{1,0:T(8,128)(2,1)S(1)}, bf16[8,192]{1,0:T(8,128)(2,1)}, u32[]{:S(2)}) copy-start(bf16[8,192]{1,0:T(8,128)(2,1)} %param.39) | copy-start | bytes 9220
  7.2 20.8 %copy-start.5 = (bf16[1024,768]{1,0:T(8,128)(2,1)S(1)}, bf16[1024,768]{1,0:T(8,128)(2,1)}, u32[]{:S(2)}) copy-start(bf16[1024,768]{1,0:T(8,128)(2,1)} %param.23) | copy-start | bytes 4718596
  7.2 61.6 %all-gather.15.cloned.1.call-start = ((), (), s32[]{:S(2)}) async-start(), calls=%async_computation.2 | async-start | bytes 1622016 | tf_op jit(solution)/shard_map/all_gather | solution.py:72
  8.0 117.8 %all-gather.13.cloned.1.call-start = ((), (), s32[]{:S(2)}) async-start(), calls=%async_computation.1 | async-start | bytes 1622016 | tf_op jit(solution)/shard_map/all_gather | solution.py:72
  8.7 174.0 %all-gather.11.cloned.1.call-start = ((), (), s32[]{:S(2)}) async-start(), calls=%async_computation | async-start | bytes 1622016 | tf_op jit(solution)/shard_map/all_gather | solution.py:72
  9.4 230.0 %all-gather.17.cloned.1.call-start = ((), (), s32[]{:S(2)}) async-start(), calls=%async_computation.3 | async-start | bytes 1622016 | tf_op jit(solution)/shard_map/all_gather | solution.py:72
  11.0 293.7 %all-gather.21.cloned.1.call-start = ((), (), s32[]{:S(2)}) async-start(), calls=%async_computation.5 | async-start | bytes 4866048 | tf_op jit(solution)/shard_map/all_gather | solution.py:72
  11.6 358.4 %all-gather.19.cloned.1.call-start = ((), (), s32[]{:S(2)}) async-start(), calls=%async_computation.4 | async-start | bytes 4866048 | tf_op jit(solution)/shard_map/all_gather | solution.py:72
  12.2 566.7 %all-gather.23.cloned.1.call-start = ((), (), s32[]{:S(2)}) async-start(), calls=%async_computation.6 | async-start | bytes 1622016 | tf_op jit(solution)/shard_map/all_gather | solution.py:154
  12.2 17.5 %copy-start.42 = (u32[32]{0:T(128)S(1)}, u32[32]{0:T(128)}, u32[]{:S(2)}) copy-start(u32[32]{0:T(128)} %constant.103) | copy-start | bytes 388
  12.3 18.7 %copy-start.36 = (f32[192]{0:T(256)S(1)}, f32[192]{0:T(256)}, u32[]{:S(2)}) copy-start(f32[192]{0:T(256)} %param.31) | copy-start | bytes 2308
  12.3 18.9 %copy-start.37 = (f32[192]{0:T(256)S(1)}, f32[192]{0:T(256)}, u32[]{:S(2)}) copy-start(f32[192]{0:T(256)} %param.32) | copy-start | bytes 2308
  14.9 31.0 %copy-start.29 = (bf16[768,8]{0,1:T(8,128)(2,1)S(1)}, bf16[768,8]{0,1:T(8,128)(2,1)}, u32[]{:S(2)}) copy-start(bf16[768,8]{0,1:T(8,128)(2,1)} %param.37) | copy-start | bytes 36868
  22.6 109.6 %copy-start.25 = (bf16[768,8]{0,1:T(8,128)(2,1)}, bf16[768,8]{0,1:T(8,128)(2,1)S(1)}, u32[]{:S(2)}) copy-start(bf16[768,8]{0,1:T(8,128)(2,1)S(1)} %reshape.204) | copy-start | bytes 36868
  28.1 161.0 %copy-start.27 = (bf16[768,8]{0,1:T(8,128)(2,1)}, bf16[768,8]{0,1:T(8,128)(2,1)S(1)}, u32[]{:S(2)}) copy-start(bf16[768,8]{0,1:T(8,128)(2,1)S(1)} %reshape.202) | copy-start | bytes 36868
  45.9 86.3 %copy-start.21 = (bf16[1024,8]{0,1:T(8,128)(2,1)}, bf16[1024,8]{0,1:T(8,128)(2,1)S(1)}, u32[]{:S(2)}) copy-start(bf16[1024,8]{0,1:T(8,128)(2,1)S(1)} %convolution_convert_fusion.4) | copy-start | bytes 49156
  46.4 142.6 %copy-start.23 = (bf16[1024,8]{0,1:T(8,128)(2,1)}, bf16[1024,8]{0,1:T(8,128)(2,1)S(1)}, u32[]{:S(2)}) copy-start(bf16[1024,8]{0,1:T(8,128)(2,1)S(1)} %convolution_convert_fusion.5) | copy-start | bytes 49156
  78.7 115.6 %copy-start.8 = (bf16[2,512,12,64]{1,0,3,2:T(2,128)(2,1)}, bf16[2,512,12,64]{1,0,3,2:T(2,128)(2,1)S(1)}, u32[]{:S(2)}) copy-start(bf16[2,512,12,64]{1,0,3,2:T(2,128)(2,1)S(1)} %reshape.183) | copy-start | bytes 4718596
  130.7 1.4 copy-start.15
  187.6 1.4 copy-start.17
  194.3 25.0 %copy-start.3 = (bf16[2,512,12,64]{1,0,3,2:T(2,128)(2,1)}, bf16[2,512,12,64]{1,0,3,2:T(2,128)(2,1)S(1)}, u32[]{:S(2)}) copy-start(bf16[2,512,12,64]{1,0,3,2:T(2,128)(2,1)S(1)} %reshape.177) | copy-start | bytes 4718596
  209.0 10.2 %copy-start.19 = (f32[2,12,512]{2,1,0:T(8,128)}, f32[2,12,512]{2,1,0:T(8,128)S(1)}, u32[]{:S(2)}) copy-start(f32[2,12,512]{2,1,0:T(8,128)S(1)} %get-tuple-element.29) | copy-start | bytes 147460
  219.2 4.5 copy-start.1
  226.9 15.4 %copy-start.38 = (f32[768]{0:T(1024)S(1)}, f32[768]{0:T(1024)}, u32[]{:S(2)}) copy-start(f32[768]{0:T(1024)} %param.33) | copy-start | bytes 9220
  242.3 4.0 copy-start.18
  246.3 215.6 %copy-start.6 = (f32[1024,768]{0,1:T(8,128)}, f32[1024,768]{0,1:T(8,128)S(1)}, u32[]{:S(2)}) copy-start(f32[1024,768]{0,1:T(8,128)S(1)} %get-tuple-element.32) | copy-start | bytes 9437188
  370.1 6.7 %copy-start.40 = (f32[768]{0:T(1024)S(1)}, f32[768]{0:T(1024)}, u32[]{:S(2)}) copy-start(f32[768]{0:T(1024)} %param.41) | copy-start | bytes 9220
  370.1 6.7 %copy-start.41 = (f32[768]{0:T(1024)S(1)}, f32[768]{0:T(1024)}, u32[]{:S(2)}) copy-start(f32[768]{0:T(1024)} %param.40) | copy-start | bytes 9220
  376.7 36.2 %copy-start.39 = (f32[768]{0:T(1024)S(1)}, f32[768]{0:T(1024)}, u32[]{:S(2)}) copy-start(f32[768]{0:T(1024)} %param.35) | copy-start | bytes 9220
  430.0 2.8 copy-start.7
  430.0 2.8 copy-start.31
  430.0 2.8 copy-start.32
  467.5 5.7 copy-start.4
  486.0 9.7 %copy-start.10 = (bf16[1024,768]{0,1:T(8,128)(2,1)S(1)}, bf16[1024,768]{0,1:T(8,128)(2,1)}, u32[]{:S(2)}) copy-start(bf16[1024,768]{0,1:T(8,128)(2,1)} %get-tuple-element.26) | copy-start | bytes 4718596
  495.8 1.6 copy-start.20
  497.3 17.1 %copy-start.9 = (bf16[2,512,12,64]{1,0,3,2:T(2,128)(2,1)S(1)}, bf16[2,512,12,64]{1,0,3,2:T(2,128)(2,1)}, u32[]{:S(2)}) copy-start(bf16[2,512,12,64]{1,0,3,2:T(2,128)(2,1)} %copy-done.8) | copy-start | bytes 4718596
  514.5 4.5 copy-start.2
  519.0 2.0 copy-start.11
  521.1 2.1 copy-start.24
  533.8 3.2 copy-start.26
  539.4 4.7 copy-start.16
  544.2 3.2 copy-start.12
  544.2 3.2 copy-start.14
  547.4 3.2 copy-start.28
  547.4 3.2 copy-start.30
  (2 other events, 2.0 us)
Sparse Core Ops, SparseCore 0:
  11.0 57.8 all-gather.14
  71.7 53.9 all-gather.12
  128.7 53.9 all-gather.10
  185.4 53.9 all-gather.16
  242.2 62.5 all-gather.20
  307.5 62.4 all-gather.18
  524.9 53.8 all-gather.22
